TPU v7x, 128 devices: a whole 4x4x4 slice. The times are simulated.
128 devices in a mesh: dp: 4 (over y), fsdp: 4 (over x_lo, core), ctx: 8 (over z, x_hi).
Axes of the slice: x: 4 (x_hi: 2, x_lo: 2; x = x_hi * 2 + x_lo), y: 4, z: 4, core: 2. Of those that a mesh axis runs over, the one named last changes fastest.
Arguments:
- tokens: bfloat16 [16, 4096, 1024], P(('dp', 'fsdp'), 'ctx')
- bounds: int32 [16, 4096], P(('dp', 'fsdp'), 'ctx'), may hold values 0 or 1
- decay_rates: float32 [16], replicated, may hold values from 2.4414063e-05 to 0.9
- w_query: bfloat16 [1024, 1024], P('fsdp')
- w_key: bfloat16 [1024, 1024], P('fsdp')
- w_up: bfloat16 [1024, 2048], P('fsdp'), may hold values from -0.1875 to 0.1875
- grad_out: bfloat16 [16, 4096, 2048], P(('dp', 'fsdp'), 'ctx'), may hold values from -6 to 6
Outputs:
- dechunked: bfloat16 [16, 4096, 2048], P(('dp', 'fsdp'), 'ctx')
- grad_tokens: bfloat16 [16, 4096, 1024], P(('dp', 'fsdp'), 'ctx')
- grad_query: float32 [1024, 1024], P('fsdp')
- grad_key: float32 [1024, 1024], P('fsdp')
- grad_up: float32 [1024, 2048], P('fsdp')
All inputs are finite; a program needn't handle non-finite values. No bound on the sum of `bounds` on one device may be relied on, other than what follows from the above.
Results may differ from a plain program's by a relative error of at most 0.0049.
Values may be sent and summed in bfloat16 or wider, within the bound.
No kernel may reach another device: no remote copies, remote signals or barrier semaphores. Data moves between devices by JAX's collectives and lax.ppermute only.
A program may use at most 128 MiB of HBM per device.

v0:
```python
import jax
import jax.numpy as jnp
from jax import lax
from jax.sharding import PartitionSpec as P

SPAN = 128
epsilon = 1e-06


def shifted(x, axis, by):
    devices = lax.axis_size(axis)
    pairs = [(i, i + by) for i in range(devices) if 0 <= i + by < devices]
    return lax.ppermute(x, axis, pairs)


def carried_in(part, axis, combine, identity, reverse):
    count = lax.axis_size(axis)
    place = lax.axis_index(axis)
    ahead = count - 1 - place if reverse else place
    gathered = jax.tree.map(lambda a: lax.all_gather(a, axis), part)
    state = jax.tree.map(lambda a, e: jnp.zeros_like(a) + jnp.asarray(e, a.dtype), part, identity)

    def one(turn, state):
        source = count - 1 - turn if reverse else turn
        return combine(
            state, jax.tree.map(lambda a: lax.dynamic_index_in_dim(a, source, 0, False), gathered)
        )

    return lax.fori_loop(0, ahead, one, state)


def chain_pair(earlier, latter):
    decay_first, state_first = earlier
    decay_second, state_second = latter
    return (decay_first * decay_second, decay_second[..., None] * state_first + state_second)


def per_device(tokens, bounds, decay_rates, w_query, w_key, w_up, grad_out):
    batch_local, length, model_width = tokens.shape
    hidden = w_up.shape[1]
    head_count = decay_rates.shape[0]
    channels = hidden // head_count
    blocks = length // SPAN
    columns_all = 2 * model_width + hidden
    flat_tokens = tokens.reshape(batch_local * length, model_width)
    panels = jnp.concatenate([w_query, w_key, w_up], 1)
    full_panels = lax.all_gather(panels, "fsdp", axis=0, tiled=True)
    projected = jnp.dot(flat_tokens, full_panels, preferred_element_type=jnp.float32)
    queries = projected[:, :model_width].reshape(batch_local, length, model_width)
    keys_now = projected[:, model_width : 2 * model_width].reshape(batch_local, length, model_width)
    values = projected[:, 2 * model_width :].reshape(
        batch_local, blocks, SPAN, head_count, channels
    )
    key_before = shifted(keys_now[:, -1:, :], "ctx", 1)
    keys_prev = jnp.concatenate([key_before, keys_now[:, :-1]], 1)
    inv_query = lax.rsqrt(jnp.sum(queries * queries, -1) + epsilon)
    inv_key = lax.rsqrt(jnp.sum(keys_prev * keys_prev, -1) + epsilon)
    cosine = jnp.sum(queries * keys_prev, -1) * inv_query * inv_key
    own_index = lax.axis_index("ctx")
    opening = jnp.logical_and(own_index == 0, jnp.arange(length) == 0)[None, :]
    boundary_prob = jnp.where(opening, 1.0, 0.5 * (1.0 - cosine))
    marked = jnp.where(opening, 1.0, bounds.astype(jnp.float32))
    mix_rate = (marked * boundary_prob)[..., None] * decay_rates
    rate_blocks = mix_rate.reshape(batch_local, blocks, SPAN, head_count)
    log_keep = jnp.cumsum(jnp.log(1.0 - rate_blocks), axis=2)
    keep_heads = jnp.moveaxis(log_keep, 3, 2)
    log_gap = keep_heads[..., :, None] - keep_heads[..., None, :]
    offsets = jnp.arange(SPAN)
    lower_mask = offsets[:, None] >= offsets[None, :]
    upper_mask = offsets[:, None] <= offsets[None, :]
    forward_band = (
        jnp.where(lower_mask, jnp.exp(jnp.where(lower_mask, log_gap, -1e30)), 0.0)
        * jnp.moveaxis(rate_blocks, 3, 2)[..., None, :]
    )
    local_states = jnp.einsum(
        "bnhtu,bnuhc->bnthc", forward_band, values, precision=lax.Precision.HIGHEST
    )
    block_logs = log_keep[:, :, -1]
    block_decay = jnp.exp(block_logs)
    running_logs = jnp.cumsum(block_logs, axis=1)
    decay_before = jnp.exp(running_logs - block_logs)
    decay_after = jnp.exp(running_logs[:, -1:] - running_logs)
    device_decay = jnp.exp(running_logs[:, -1])
    inner_zero = jnp.zeros((batch_local, head_count, channels), jnp.float32)

    def walk_blocks(carried, element):
        decay_now, addition = element
        return (decay_now[..., None] * carried + addition, carried)

    device_state, block_in = lax.scan(
        walk_blocks,
        inner_zero,
        (jnp.moveaxis(block_decay, 1, 0), jnp.moveaxis(local_states[:, :, -1], 1, 0)),
    )
    identity_pair = (jnp.ones_like(device_decay), inner_zero)
    _, state_in = carried_in((device_decay, device_state), "ctx", chain_pair, identity_pair, False)
    block_carry = jnp.moveaxis(block_in, 0, 1) + decay_before[..., None] * state_in[:, None]
    states = local_states + jnp.exp(log_keep)[..., None] * block_carry[:, :, None]
    dechunked = states.reshape(batch_local, length, hidden).astype(jnp.bfloat16)
    state_rows = states.reshape(batch_local, length, head_count, channels)
    states_prev = jnp.concatenate([state_in[:, None], state_rows[:, :-1]], 1)
    cotangent = grad_out.astype(jnp.float32).reshape(
        batch_local, blocks, SPAN, head_count, channels
    )
    backward_band = jnp.where(upper_mask, jnp.exp(jnp.where(upper_mask, -log_gap, -1e30)), 0.0)
    local_adjoint = jnp.einsum(
        "bnhtu,bnuhc->bnthc", backward_band, cotangent, precision=lax.Precision.HIGHEST
    )
    block_heads = (1.0 - rate_blocks[:, :, 0])[..., None] * local_adjoint[:, :, 0]
    device_head, block_out = lax.scan(
        walk_blocks,
        inner_zero,
        (jnp.moveaxis(block_decay, 1, 0), jnp.moveaxis(block_heads, 1, 0)),
        reverse=True,
    )
    _, adjoint_in = carried_in((device_decay, device_head), "ctx", chain_pair, identity_pair, True)
    block_from = jnp.moveaxis(block_out, 0, 1) + decay_after[..., None] * adjoint_in[:, None]
    adjoints = (
        local_adjoint + jnp.exp(log_keep[:, :, -1:] - log_keep)[..., None] * block_from[:, :, None]
    )
    adjoint_rows = adjoints.reshape(batch_local, length, head_count, channels)
    d_values = (
        (mix_rate[..., None] * adjoint_rows)
        .reshape(batch_local, length, hidden)
        .astype(jnp.bfloat16)
    )
    value_rows = values.reshape(batch_local, length, head_count, channels)
    d_rate = jnp.sum(adjoint_rows * (value_rows - states_prev), -1)
    d_prob = jnp.where(opening, 0.0, marked * jnp.sum(d_rate * decay_rates, -1))
    d_cos = -0.5 * d_prob
    pair_scale = inv_query * inv_key
    d_query = (
        d_cos[..., None]
        * (
            keys_prev * pair_scale[..., None]
            - (cosine * inv_query * inv_query)[..., None] * queries
        )
    ).astype(jnp.bfloat16)
    d_prev = d_cos[..., None] * (
        queries * pair_scale[..., None] - (cosine * inv_key * inv_key)[..., None] * keys_prev
    )
    key_after = shifted(d_prev[:, :1, :], "ctx", -1)
    d_key = jnp.concatenate([d_prev[:, 1:], key_after], 1).astype(jnp.bfloat16)
    d_all = jnp.concatenate([d_query, d_key, d_values], 2).reshape(
        batch_local * length, columns_all
    )
    d_flat = lax.dot_general(
        d_all, full_panels, (((1,), (1,)), ((), ())), preferred_element_type=jnp.float32
    )
    grad_tokens = d_flat.reshape(batch_local, length, model_width).astype(jnp.bfloat16)
    grads = lax.dot_general(
        flat_tokens, d_all, (((0,), (0,)), ((), ())), preferred_element_type=jnp.float32
    )
    reduced = lax.psum_scatter(grads, "fsdp", scatter_dimension=0, tiled=True)
    summed = lax.psum(reduced, ("dp", "ctx"))
    return (
        dechunked,
        grad_tokens,
        summed[:, :model_width],
        summed[:, model_width : 2 * model_width],
        summed[:, 2 * model_width :],
    )


def solution(mesh):
    return jax.shard_map(
        per_device,
        mesh=mesh,
        in_specs=(
            P(("dp", "fsdp"), "ctx", None),
            P(("dp", "fsdp"), "ctx"),
            P(),
            P("fsdp", None),
            P("fsdp", None),
            P("fsdp", None),
            P(("dp", "fsdp"), "ctx", None),
        ),
        out_specs=(
            P(("dp", "fsdp"), "ctx", None),
            P(("dp", "fsdp"), "ctx", None),
            P("fsdp", None),
            P("fsdp", None),
            P("fsdp", None),
        ),
        check_vma=False,
    )
```

profile of v0, /device:TPU:0, one launch (start us, length us, event | category | flops | bytes accessed | tf_op | source)
XLA Modules:
  0.0 855.9 jit_solution(13481682281090934830)
XLA Ops:
  7.2 3.2 pad_maximum_fusion.2
  10.5 2.0 copy.154
  12.5 0.6 iota_compare_fusion
  13.1 79.9 %all-gather.4.cloned.1.call-done = bf16[1024,4096]{1,0:T(8,128)(2,1)} async-done(((bf16[256,4096]{1,0:T(8,128)(2,1)}), bf16[1024,4096]{1,0:T(8,128)(2,1)}) %all-gather.4.cloned.1.call-update) | async-done | bytes 8388624 | tf_op jit(solution)/shard_map/all_gather | solution.py:47
  93.1 6.9 convolution_bitcast_fusion.1
  100.7 4.6 collective-permute-start
  105.6 2.9 copy.153
  109.4 0.6 multiply_multiply_fusion.1
  110.2 0.8 copy.129
  111.0 1.2 reduce_window_sum.26
  112.9 0.6 copy-done.16
  113.6 7.8 fusion.21
  121.4 1.9 copy-done.6
  123.4 2.9 while.58
  123.4 0.6 fusion.66
  124.8 0.7 fusion.66
  125.6 0.7 fusion.66
  126.3 34.6 %all-gather = f32[8,16,128]{2,1,0:T(8,128)S(1)} all-gather(f32[1,16,128]{2,1,0:T(8,128)S(1)} %get-tuple-element.266), channel_id=2, replica_groups=mesh['dp'=4,'fsdp'=4,'ctx'=8] {'ctx'}, dimensions={0}, use_global_device_ids=true | all-gather | bytes 73728 | tf_op jit(solution)/shard_map/all_gather | solution.py:20
  161.0 0.7 reduce_window_sum.28
  162.2 22.3 %all_gather.22 = f32[8,1,16]{2,1,0:T(1,128)} all-gather(f32[1,1,16]{2,1,0:T(1,128)S(1)} %get-tuple-element.521), channel_id=1, replica_groups=mesh['dp'=4,'fsdp'=4,'ctx'=8] {'ctx'}, dimensions={0}, use_global_device_ids=true | all-gather | bytes 576 | tf_op jit(solution)/shard_map/all_gather | solution.py:20
  184.5 1.5 fusion.50
  186.1 1.3 fusion.53
  187.4 5.0 fusion.18
  192.4 2.0 copy-done.7
  194.6 2.9 while.59
  194.6 0.7 fusion.67
  195.3 0.7 fusion.67
  196.8 0.6 fusion.67
  197.5 35.0 %all-gather.1 = f32[8,16,128]{2,1,0:T(8,128)S(1)} all-gather(f32[1,16,128]{2,1,0:T(8,128)S(1)} %get-tuple-element.269), channel_id=3, replica_groups=mesh['dp'=4,'fsdp'=4,'ctx'=8] {'ctx'}, dimensions={0}, use_global_device_ids=true | all-gather | bytes 73728 | tf_op jit(solution)/shard_map/all_gather | solution.py:20
  232.5 5.4 while.57
  232.5 0.6 dynamic-slice_bitcast_fusion.5
  233.2 0.7 dynamic-slice_bitcast_fusion.5
  235.3 0.6 dynamic-slice_bitcast_fusion.5
  236.0 0.7 dynamic-slice_bitcast_fusion.5
  238.0 0.8 bitcast_add_fusion.4
  238.8 3.8 fusion.59
  242.6 2.4 copy.143
  245.1 2.2 slice.76
  247.4 2.6 pad_maximum_fusion.1
  250.0 0.8 copy-done.3
  250.9 1.3 copy-done.8
  252.2 3.8 fusion.16
  256.2 2.1 multiply_bitcast_fusion
  258.3 1.0 copy-done.9
  259.2 1.3 collective-permute-start.1
  260.5 4.4 copy.146
  265.0 2.8 mul.510
  267.8 9.8 %multiply_convert_fusion = bf16[1,512,2048]{2,0,1:T(2,128)(2,1)} fusion(f32[1,512,2048]{2,0,1:T(1,128)} %bitcast.151, f32[1,512,2048]{2,0,1:T(1,128)} %bitcast.150), kind=kLoop, calls=%fused_computation.34 | loop fusion | flops 2097152 | bytes 10485760 | tf_op jit(solution)/shard_map/convert_element_type | solution.py:125
  277.6 2.2 fusion.47
  280.1 1.6 copy.147
  281.8 1.6 copy.148
  283.4 9.9 %pad_maximum_fusion = bf16[1,512,4096]{2,0,1:T(2,128)(2,1)S(1)} fusion(bf16[1,512,2048]{2,0,1:T(2,128)(2,1)S(1)} %copy-done.2, bf16[1,512,1024]{2,0,1:T(2,128)(2,1)S(1)} %copy.148, bf16[1,512,1024]{2,0,1:T(2,128)(2,1)S(1)} %copy.147), kind=kLoop, calls=%fused_computation.13 | loop fusion | flops 12582912 | bytes 8388608 | tf_op jit(solution)/shard_map/concatenate | solution.py:144
  293.3 3.2 copy-done.5
  296.6 15.4 %convolution_bitcast_fusion = f32[1024,4096]{0,1:T(8,128)} fusion(bf16[1,512,4096]{2,0,1:T(2,128)(2,1)S(1)} %pad_maximum_fusion, bf16[1,512,1024]{2,1,0:T(8,128)(2,1)S(1)} %copy-done), kind=kOutput, calls=%fused_computation.12 | convolution fusion | flops 4294967296 | bytes 22020096 | tf_op jit(solution)/shard_map/dot_general | solution.py:151
  312.1 146.3 %reduce-scatter.2.cloned.1.call-done = f32[256,4096]{0,1:T(8,128)} async-done(((f32[1024,4096]{0,1:T(8,128)}), f32[256,4096]{0,1:T(8,128)}) %reduce-scatter.2.cloned.1.call-update) | async-done | bytes 4194320 | tf_op jit(solution)/shard_map/reduce_scatter | solution.py:154
  458.4 2.7 copy.137
  461.1 4.4 convert_element_type.52
  465.4 14.2 %fusion.44 = bf16[1,512,1024]{2,1,0:T(8,128)(2,1)} fusion(bf16[1024,4096]{1,0:T(8,128)(2,1)} %all-gather.4.cloned.1.call-done, bf16[1,512,4096]{2,0,1:T(2,128)(2,1)} %copy-done.5), kind=kOutput, calls=%fused_computation.64 | convolution fusion | flops 4295491584 | bytes 13631488 | tf_op jit(solution)/shard_map/dot_general | solution.py:147
  479.7 361.8 %all-reduce.2.cloned.1.call-done = f32[256,4096]{0,1:T(8,128)} async-done(((f32[256,4096]{0,1:T(8,128)}), f32[256,4096]{0,1:T(8,128)}) %all-reduce.2.cloned.1.call-update) | async-done | bytes 4194320 | tf_op jit(solution)/shard_map/psum | solution.py:155
  841.4 1.6 slice-done
  843.0 1.8 copy.151
  844.8 1.7 fusion.60
  846.5 1.3 copy.149
  847.8 1.3 copy.150
  (115 shorter events, 8.7 us)
Async XLA Ops:
  7.2 85.9 %copy-start = (bf16[1,512,1024]{2,1,0:T(8,128)(2,1)S(1)}, bf16[1,512,1024]{2,1,0:T(8,128)(2,1)}, u32[]{:S(2)}) copy-start(bf16[1,512,1024]{2,1,0:T(8,128)(2,1)} %param.15) | copy-start | bytes 3145732
  7.2 3.4 copy-start.11
  7.2 85.9 %all-gather.4.cloned.1.call-start = ((), (), s32[]{:S(2)}) async-start(), calls=%async_computation.1 | async-start | bytes 10485760 | tf_op jit(solution)/shard_map/all_gather | solution.py:47
  10.5 447.9 %reduce-scatter.2.cloned.1.call-start = ((), (), s32[]{:S(2)}) async-start(), calls=%async_computation.2 | async-start | bytes 20971520 | tf_op jit(solution)/shard_map/reduce_scatter | solution.py:154
  100.0 8.6 copy-start.1
  100.7 7.8 collective-permute-start
  108.5 1.6 copy-start.23
  108.5 1.6 copy-start.25
  108.5 1.6 copy-start.14
  110.1 2.8 copy-start.18
  112.9 0.6 copy-start.16
  121.4 1.9 copy-start.6
  161.7 22.8 %copy-start.22 = (f32[1,4,16]{2,1,0:T(4,128)}, f32[1,4,16]{2,1,0:T(4,128)S(1)}, u32[]{:S(2)}) copy-start(f32[1,4,16]{2,1,0:T(4,128)S(1)} %reduce_window_sum.28) | copy-start | bytes 772
  187.4 50.5 %copy-start.13 = (f32[4,128,16]{2,1,0:T(8,128)S(1)}, f32[4,128,16]{2,1,0:T(8,128)}, u32[]{:S(2)}) copy-start(f32[4,128,16]{2,1,0:T(8,128)} %get-tuple-element.508) | copy-start | bytes 98308
  192.4 2.0 copy-start.7
  245.1 2.2 copy-start.12
  247.4 3.5 copy-start.3
  247.4 4.7 copy-start.8
  252.1 3.9 copy-start.26
  252.1 4.0 copy-start.24
  252.1 4.0 copy-start.15
  252.1 4.0 copy-start.17
  252.1 4.0 copy-start.21
  258.3 1.0 copy-start.9
  259.2 22.5 %collective-permute-start.1 = (bf16[1,1,1024]{2,1,0:T(2,128)(2,1)S(1)}, bf16[1,1,1024]{2,1,0:T(2,128)(2,1)S(1)}, u32[]{:S(2)}, u32[]{:S(2)}) collective-permute-start(bf16[1,1,1024]{2,1,0:T(2,128)(2,1)S(1)} %slice.78), channel_id=1, source_target_pairs={{1,0},{2,1},{3,2},{4,3},{5,4},{6,5},{7,6},{9,8},{10,9},{11,10},{12... | collective-permute-start | bytes 6152 | tf_op jit(solution)/shard_map/ppermute | solution.py:13
  260.5 4.4 copy-start.19
  267.8 9.8 %copy-start.20 = (f32[512]{0:T(512)S(1)}, f32[512]{0:T(512)}, u32[]{:S(2)}) copy-start(f32[512]{0:T(512)} %get-tuple-element.511) | copy-start | bytes 6148
  277.6 2.2 copy-start.10
  280.0 3.4 copy-start.2
  293.3 3.2 copy-start.5
  312.0 146.4 %copy-start.4 = (bf16[1,4,128,16,128]{4,2,3,1,0:T(8,128)(2,1)S(1)}, bf16[1,4,128,16,128]{4,2,3,1,0:T(8,128)(2,1)}, u32[]{:S(2)}) copy-start(bf16[1,4,128,16,128]{4,2,3,1,0:T(8,128)(2,1)} %get-tuple-element.501) | copy-start | bytes 6291460
  312.0 529.4 %all-reduce.2.cloned.1.call-start = ((), (), s32[]{:S(2)}) async-start(), calls=%async_computation.3 | async-start | bytes 8388608 | tf_op jit(solution)/shard_map/psum | solution.py:155
  841.4 1.6 slice-start
Sparse Core Ops, SparseCore 0:
  10.6 82.4 all-gather.3
  312.1 146.1 reduce-scatter.1
  460.9 380.5 all-reduce.1
where the time goes:
time: 864 us; the launch traced here: 856 us
  waiting for transfers between devices  588 us (68%)
  blocking collectives  92 us (11%)
  local copies, waits for them, and re-layouts  58.6 us (7%)
  matrix products  49.4 us (6%)
  other arithmetic  46.9 us (5%)
  between operations  14.5 us (2%)
    psum x1, waiting for transfers between devices, per_device(): summed = lax.psum(reduced, ('dp', 'ctx'))  362 us
    reduce_scatter x1, waiting for transfers between devices, per_device(): reduced = lax.psum_scatter(grads, 'fsdp', scatter_dimension=0, tiled=True)  146 us
    all_gather x3, blocking collectives, carried_in(): gathered = jax.tree.map(lambda a: lax.all_gather(a, axis), part)  92 us
    all_gather x1, waiting for transfers between devices, per_device(): full_panels = lax.all_gather(panels, 'fsdp', axis=0, tiled=True)  79.9 us
    unnamed x60, local copies, waits for them, and re-layouts  20.7 us
  transfers between devices with their start and end apart: 5, of which 3 were waited for; matrix products, arithmetic and copies ran while one was open for 6% of the time, Pallas kernels for 0%

commit v1 on v0

--- a/solution.py
+++ b/solution.py
@@ -152,7 +152,9 @@
         flat_tokens, d_all, (((0,), (0,)), ((), ())), preferred_element_type=jnp.float32
     )
     reduced = lax.psum_scatter(grads, "fsdp", scatter_dimension=0, tiled=True)
-    summed = lax.psum(reduced, ("dp", "ctx"))
+    summed = reduced
+    for q in ("dp", "ctx"):
+        summed = lax.psum(summed, q)
     return (
         dechunked,
         grad_tokens,

time: 864 us -> 765 us (0.89)
  waiting for transfers between devices: 588 us -> 488 us
    psum x1 -> x2, waiting for transfers between devices: 362 us -> 262 us  [per_device(): summed = lax.psum(summed, q)]
  transfers between devices with their start and end apart: 5 -> 6, of which waited for: 3 -> 4; matrix products, arithmetic and copies ran while one was open for 6% -> 6% of each run, Pallas kernels for 0% -> 0%
where the time goes in v1:
time: 765 us; the launch traced here: 756 us
  waiting for transfers between devices  488 us (64%)
  blocking collectives  92 us (12%)
  local copies, waits for them, and re-layouts  58.6 us (8%)
  matrix products  49.7 us (6%)
  other arithmetic  46.9 us (6%)
  between operations  14.5 us (2%)
    psum x2, waiting for transfers between devices, per_device(): summed = lax.psum(summed, q)  262 us
    reduce_scatter x1, waiting for transfers between devices, per_device(): reduced = lax.psum_scatter(grads, 'fsdp', scatter_dimension=0, tiled=True)  146 us
    all_gather x3, blocking collectives, carried_in(): gathered = jax.tree.map(lambda a: lax.all_gather(a, axis), part)  92 us
    all_gather x1, waiting for transfers between devices, per_device(): full_panels = lax.all_gather(panels, 'fsdp', axis=0, tiled=True)  79.9 us
    unnamed x60, local copies, waits for them, and re-layouts  20.7 us
    dot_general x1, matrix products, per_device(): lax.dot_general(flat_tokens, d_all, (((0,), (0,)), ((), ())), preferred_e...  15.4 us
  transfers between devices with their start and end apart: 6, of which 4 were waited for; matrix products, arithmetic and copies ran while one was open for 6% of the time, Pallas kernels for 0%

profile of v1, /device:TPU:0, one launch (start us, length us, event | category | flops | bytes accessed | tf_op | source)
XLA Modules:
  0.0 756.4 jit_solution(11619156326138579012)
XLA Ops:
  7.2 3.2 pad_maximum_fusion.2
  10.5 2.0 copy.154
  13.1 79.9 %all-gather.4.cloned.1.call-done = bf16[1024,4096]{1,0:T(8,128)(2,1)} async-done(((bf16[256,4096]{1,0:T(8,128)(2,1)}), bf16[1024,4096]{1,0:T(8,128)(2,1)}) %all-gather.4.cloned.1.call-update) | async-done | bytes 8388624 | tf_op jit(solution)/shard_map/all_gather | solution.py:47
  93.1 6.9 convolution_bitcast_fusion.1
  100.7 4.6 collective-permute-start
  105.6 2.9 copy.153
  109.4 0.6 multiply_multiply_fusion.1
  110.2 0.8 copy.129
  111.0 1.2 reduce_window_sum.26
  112.9 0.6 copy-done.16
  113.6 7.8 %fusion.21 = f32[1,4,128,16,128]{4,2,3,1,0:T(8,128)S(1)} fusion(f32[4,128,16,128]{3,2,1,0:T(8,128)} %bitcast.152, f32[4,16,128]{2,1,0:T(8,128)S(1)} %get-tuple-element.516, f32[4,16,128]{2,1,0:T(8,128)S(1)} %copy.130, pred[128,128]{1,0:T(8,128)(4,1)S(1)} %iota_compare_fusion.1), kind=kOutput, calls=%fused_computation.38 | convolution fusion | flops 1614807040 | bytes 8470528 | tf_op jit(solution)/shard_map/bnhtu,bnuhc->bnthc/dot_general | solution.py:75
  121.4 1.9 copy-done.6
  123.4 2.9 while.58
  123.4 0.6 fusion.66
  124.8 0.7 fusion.66
  125.6 0.7 fusion.66
  126.3 34.6 %all-gather = f32[8,16,128]{2,1,0:T(8,128)S(1)} all-gather(f32[1,16,128]{2,1,0:T(8,128)S(1)} %get-tuple-element.266), channel_id=2, replica_groups=mesh['dp'=4,'fsdp'=4,'ctx'=8] {'ctx'}, dimensions={0}, use_global_device_ids=true | all-gather | bytes 73728 | tf_op jit(solution)/shard_map/all_gather | solution.py:20
  161.0 0.7 reduce_window_sum.28
  162.2 22.3 %all_gather.22 = f32[8,1,16]{2,1,0:T(1,128)} all-gather(f32[1,1,16]{2,1,0:T(1,128)S(1)} %get-tuple-element.521), channel_id=1, replica_groups=mesh['dp'=4,'fsdp'=4,'ctx'=8] {'ctx'}, dimensions={0}, use_global_device_ids=true | all-gather | bytes 576 | tf_op jit(solution)/shard_map/all_gather | solution.py:20
  184.5 1.5 fusion.50
  186.1 1.3 fusion.53
  187.4 5.0 fusion.18
  192.4 2.0 copy-done.7
  194.6 2.9 while.59
  194.6 0.7 fusion.67
  195.3 0.7 fusion.67
  196.8 0.6 fusion.67
  197.5 35.0 %all-gather.1 = f32[8,16,128]{2,1,0:T(8,128)S(1)} all-gather(f32[1,16,128]{2,1,0:T(8,128)S(1)} %get-tuple-element.269), channel_id=3, replica_groups=mesh['dp'=4,'fsdp'=4,'ctx'=8] {'ctx'}, dimensions={0}, use_global_device_ids=true | all-gather | bytes 73728 | tf_op jit(solution)/shard_map/all_gather | solution.py:20
  232.5 5.4 while.57
  232.5 0.6 dynamic-slice_bitcast_fusion.5
  233.2 0.7 dynamic-slice_bitcast_fusion.5
  235.3 0.6 dynamic-slice_bitcast_fusion.5
  236.0 0.7 dynamic-slice_bitcast_fusion.5
  238.0 0.8 bitcast_add_fusion.4
  238.8 3.8 fusion.59
  242.6 2.4 copy.143
  245.1 2.2 slice.76
  247.4 2.6 pad_maximum_fusion.1
  250.0 0.8 copy-done.3
  250.9 1.3 copy-done.8
  252.2 3.8 fusion.16
  256.2 2.1 multiply_bitcast_fusion
  258.3 1.0 copy-done.9
  259.2 1.3 collective-permute-start.1
  260.5 4.4 copy.146
  265.0 2.8 mul.510
  267.8 9.8 %multiply_convert_fusion = bf16[1,512,2048]{2,0,1:T(2,128)(2,1)} fusion(f32[1,512,2048]{2,0,1:T(1,128)} %bitcast.151, f32[1,512,2048]{2,0,1:T(1,128)} %bitcast.150), kind=kLoop, calls=%fused_computation.34 | loop fusion | flops 2097152 | bytes 10485760 | tf_op jit(solution)/shard_map/convert_element_type | solution.py:125
  277.6 2.2 fusion.47
  280.1 1.6 copy.147
  281.8 1.6 copy.148
  283.4 9.9 %pad_maximum_fusion = bf16[1,512,4096]{2,0,1:T(2,128)(2,1)S(1)} fusion(bf16[1,512,2048]{2,0,1:T(2,128)(2,1)S(1)} %copy-done.2, bf16[1,512,1024]{2,0,1:T(2,128)(2,1)S(1)} %copy.148, bf16[1,512,1024]{2,0,1:T(2,128)(2,1)S(1)} %copy.147), kind=kLoop, calls=%fused_computation.13 | loop fusion | flops 12582912 | bytes 8388608 | tf_op jit(solution)/shard_map/concatenate | solution.py:144
  293.3 3.2 copy-done.5
  296.6 15.4 %convolution_bitcast_fusion = f32[1024,4096]{0,1:T(8,128)} fusion(bf16[1,512,4096]{2,0,1:T(2,128)(2,1)S(1)} %pad_maximum_fusion, bf16[1,512,1024]{2,1,0:T(8,128)(2,1)S(1)} %copy-done), kind=kOutput, calls=%fused_computation.12 | convolution fusion | flops 4294967296 | bytes 22020096 | tf_op jit(solution)/shard_map/dot_general | solution.py:151
  312.1 146.3 %reduce-scatter.2.cloned.1.call-done = f32[256,4096]{0,1:T(8,128)} async-done(((f32[1024,4096]{0,1:T(8,128)}), f32[256,4096]{0,1:T(8,128)}) %reduce-scatter.2.cloned.1.call-update) | async-done | bytes 4194320 | tf_op jit(solution)/shard_map/reduce_scatter | solution.py:154
  458.4 96.1 %all-reduce.3.cloned.1.call-done = f32[256,4096]{0,1:T(8,128)} async-done(((f32[256,4096]{0,1:T(8,128)}), f32[256,4096]{0,1:T(8,128)}) %all-reduce.3.cloned.1.call-update) | async-done | bytes 4194320 | tf_op jit(solution)/shard_map/psum | solution.py:157
  554.5 2.7 copy.137
  557.2 4.4 convert_element_type.52
  561.6 14.5 %fusion.44 = bf16[1,512,1024]{2,1,0:T(8,128)(2,1)} fusion(bf16[1024,4096]{1,0:T(8,128)(2,1)} %all-gather.4.cloned.1.call-done, bf16[1,512,4096]{2,0,1:T(2,128)(2,1)} %copy-done.5), kind=kOutput, calls=%fused_computation.64 | convolution fusion | flops 4295491584 | bytes 13631488 | tf_op jit(solution)/shard_map/dot_general | solution.py:147
  576.1 165.8 %all-reduce.5.cloned.1.call-done = f32[256,4096]{0,1:T(8,128)} async-done(((f32[256,4096]{0,1:T(8,128)}), f32[256,4096]{0,1:T(8,128)}) %all-reduce.5.cloned.1.call-update) | async-done | bytes 4194320 | tf_op jit(solution)/shard_map/psum | solution.py:157
  741.9 1.6 slice-done
  743.5 1.8 copy.151
  745.3 1.7 fusion.60
  747.0 1.3 copy.149
  748.3 1.3 copy.150
  (118 shorter events, 9.4 us)
Async XLA Ops:
  7.2 85.9 %copy-start = (bf16[1,512,1024]{2,1,0:T(8,128)(2,1)S(1)}, bf16[1,512,1024]{2,1,0:T(8,128)(2,1)}, u32[]{:S(2)}) copy-start(bf16[1,512,1024]{2,1,0:T(8,128)(2,1)} %param.15) | copy-start | bytes 3145732
  7.2 3.4 copy-start.11
  7.2 85.9 %all-gather.4.cloned.1.call-start = ((), (), s32[]{:S(2)}) async-start(), calls=%async_computation.1 | async-start | bytes 10485760 | tf_op jit(solution)/shard_map/all_gather | solution.py:47
  10.5 447.9 %reduce-scatter.2.cloned.1.call-start = ((), (), s32[]{:S(2)}) async-start(), calls=%async_computation.2 | async-start | bytes 20971520 | tf_op jit(solution)/shard_map/reduce_scatter | solution.py:154
  100.0 8.6 %copy-start.1 = (f32[512,4096]{1,0:T(8,128)}, f32[512,4096]{1,0:T(8,128)S(1)}, u32[]{:S(2)}) copy-start(f32[512,4096]{1,0:T(8,128)S(1)} %convolution_bitcast_fusion.1) | copy-start | bytes 25165828
  100.7 7.8 %collective-permute-start = (f32[1,1,1024]{2,1,0:T(1,128)S(1)}, f32[1,1,1024]{2,1,0:T(1,128)S(1)}, u32[]{:S(2)}, u32[]{:S(2)}) collective-permute-start(f32[1,1,1024]{2,1,0:T(1,128)S(1)} %slice.70), channel_id=1, source_target_pairs={{0,1},{1,2},{2,3},{3,4},{4,5},{5,6},{6,7},{8,9},{9,10},{10,11},{11... | collective-permute-start | bytes 12296 | tf_op jit(solution)/shard_map/ppermute | solution.py:13
  108.5 1.6 copy-start.23
  108.5 1.6 copy-start.25
  108.5 1.6 copy-start.14
  110.1 2.8 copy-start.18
  112.9 0.6 copy-start.16
  121.4 1.9 copy-start.6
  161.7 22.8 %copy-start.22 = (f32[1,4,16]{2,1,0:T(4,128)}, f32[1,4,16]{2,1,0:T(4,128)S(1)}, u32[]{:S(2)}) copy-start(f32[1,4,16]{2,1,0:T(4,128)S(1)} %reduce_window_sum.28) | copy-start | bytes 772
  187.4 50.5 %copy-start.13 = (f32[4,128,16]{2,1,0:T(8,128)S(1)}, f32[4,128,16]{2,1,0:T(8,128)}, u32[]{:S(2)}) copy-start(f32[4,128,16]{2,1,0:T(8,128)} %get-tuple-element.508) | copy-start | bytes 98308
  192.4 2.0 copy-start.7
  245.1 2.2 copy-start.12
  247.4 3.5 copy-start.3
  247.4 4.7 copy-start.8
  252.1 3.9 copy-start.26
  252.1 4.0 copy-start.24
  252.1 4.0 copy-start.15
  252.1 4.0 copy-start.17
  252.1 4.0 copy-start.21
  258.3 1.0 copy-start.9
  259.2 22.5 %collective-permute-start.1 = (bf16[1,1,1024]{2,1,0:T(2,128)(2,1)S(1)}, bf16[1,1,1024]{2,1,0:T(2,128)(2,1)S(1)}, u32[]{:S(2)}, u32[]{:S(2)}) collective-permute-start(bf16[1,1,1024]{2,1,0:T(2,128)(2,1)S(1)} %slice.78), channel_id=1, source_target_pairs={{1,0},{2,1},{3,2},{4,3},{5,4},{6,5},{7,6},{9,8},{10,9},{11,10},{12... | collective-permute-start | bytes 6152 | tf_op jit(solution)/shard_map/ppermute | solution.py:13
  260.5 4.4 copy-start.19
  267.8 9.8 %copy-start.20 = (f32[512]{0:T(512)S(1)}, f32[512]{0:T(512)}, u32[]{:S(2)}) copy-start(f32[512]{0:T(512)} %get-tuple-element.511) | copy-start | bytes 6148
  277.6 2.2 copy-start.10
  280.0 3.4 copy-start.2
  293.3 3.2 copy-start.5
  312.0 242.5 %all-reduce.3.cloned.1.call-start = ((), (), s32[]{:S(2)}) async-start(), calls=%async_computation.3 | async-start | bytes 8388608 | tf_op jit(solution)/shard_map/psum | solution.py:157
  458.3 96.2 %copy-start.4 = (bf16[1,4,128,16,128]{4,2,3,1,0:T(8,128)(2,1)S(1)}, bf16[1,4,128,16,128]{4,2,3,1,0:T(8,128)(2,1)}, u32[]{:S(2)}) copy-start(bf16[1,4,128,16,128]{4,2,3,1,0:T(8,128)(2,1)} %get-tuple-element.501) | copy-start | bytes 6291460
  458.4 283.6 %all-reduce.5.cloned.1.call-start = ((), (), s32[]{:S(2)}) async-start(), calls=%async_computation.4 | async-start | bytes 8388608 | tf_op jit(solution)/shard_map/psum | solution.py:157
  741.9 1.6 slice-start
Sparse Core Ops, SparseCore 0:
  10.6 82.4 all-gather.3
  312.1 146.1 reduce-scatter.1
  460.7 93.7 all-reduce.2
  556.9 185.0 all-reduce.4
